TPU v7x, 512 devices: a whole 4x4x16 slice. The times are simulated.
512 devices in a mesh: lat: 8 (over y_lo, x), lon: 64 (over z, y_hi, core).
Axes of the slice: x: 4, y: 4 (y_hi: 2, y_lo: 2; y = y_hi * 2 + y_lo), z: 16, core: 2. Of those that a mesh axis runs over, the one named last changes fastest.
Arguments:
- heights: bfloat16 [4, 2048, 32768], P(None, 'lat', 'lon'), may hold values from -24 to 24
- sigma_class: int32 [2048, 32768], P('lat', 'lon'), may hold values from 0 to 15
- window_class: int32 [2048, 32768], P('lat', 'lon'), may hold values from 0 to 15
- sigma_table: float32 [16], replicated, may hold values from 0.3 to 32, as said below
- window_table: float32 [16], replicated, may hold values from 0.3 to 32, as said below
Outputs:
- smoothed: bfloat16 [4, 2048, 32768], P(None, 'lat', 'lon')
Inputs may be any that keep to these rules, and one draw needn't show every extreme that they name: `sigma_table`: widths of the first smoothing's classes, in cells. `window_table`: widths of the second smoothing's classes, in cells.
All inputs are finite; a program needn't handle non-finite values.
Results may differ from a plain program's by a relative error of at most 0.0046.
Values may be sent and summed in bfloat16 or wider, within the bound.
No kernel may reach another device: no remote copies, remote signals or barrier semaphores. Data moves between devices by JAX's collectives and lax.ppermute only.
A program may use at most 64 MiB of HBM per device.

v0:
```python
import jax
import jax.numpy as jnp
from jax import lax
from jax.sharding import PartitionSpec as P

RADIUS = 16
NCLASS = 16


def extended(block, sides, width):
    for axis, dim in sides:
        count = lax.axis_size(axis)
        forward = [(i, i + 1) for i in range(count - 1)]
        backward = [(target, source) for source, target in forward]
        low = lax.ppermute(
            lax.slice_in_dim(block, block.shape[dim] - width, None, axis=dim), axis, forward
        )
        high = lax.ppermute(lax.slice_in_dim(block, 0, width, axis=dim), axis, backward)
        block = jnp.concatenate([low, block, high], axis=dim)
    return block


def class_weights(classes, table):
    spread_tab = 0.5 / (table * table)
    offsets = jnp.arange(-RADIUS, RADIUS + 1).astype(jnp.float32)
    norm = jnp.sum(jnp.exp(-(offsets * offsets)[None, :] * spread_tab[:, None]), axis=1)
    scale_tab = 1.0 / norm
    spread = jnp.zeros(classes.shape, jnp.float32)
    scale_cell = jnp.zeros(classes.shape, jnp.float32)
    for number in range(NCLASS):
        hit = classes == number
        spread = jnp.where(hit, spread_tab[number], spread)
        scale_cell = jnp.where(hit, scale_tab[number], scale_cell)
    return (spread, scale_cell)


def rows_pass(padded, spread, scale_cell):
    rows = spread.shape[0]
    accum = jnp.zeros((padded.shape[0],) + spread.shape, jnp.float32)
    for offset in range(-RADIUS, RADIUS + 1):
        weight = jnp.exp(-float(offset * offset) * spread)
        accum = accum + weight[None] * padded[
            :, RADIUS + offset : RADIUS + offset + rows, :
        ].astype(jnp.float32)
    return accum * scale_cell[None]


def cols_pass(padded, spread, scale_cell):
    cols = spread.shape[1]
    accum = jnp.zeros((padded.shape[0],) + spread.shape, jnp.float32)
    for offset in range(-RADIUS, RADIUS + 1):
        weight = jnp.exp(-float(offset * offset) * spread)
        accum = accum + weight[None] * padded[:, :, RADIUS + offset : RADIUS + offset + cols]
    return accum * scale_cell[None]


def smooth(field, classes, table):
    spread, scale_cell = class_weights(classes, table)
    padded = extended(field, (("lat", 1),), RADIUS)
    upper = rows_pass(padded, spread, scale_cell)
    widened = extended(upper, (("lon", 2),), RADIUS)
    result = cols_pass(widened, spread, scale_cell)
    return result.astype(jnp.bfloat16)


def per_device(heights, sigma_class, window_class, sigma_table, window_table):
    first = smooth(heights, sigma_class, sigma_table)
    return smooth(first, window_class, window_table)


def solution(mesh):
    placed = (P(None, "lat", "lon"), P("lat", "lon"), P("lat", "lon"), P(), P())
    return jax.shard_map(
        per_device, mesh=mesh, in_specs=placed, out_specs=P(None, "lat", "lon"), check_vma=False
    )
```

profile of v0, /device:TPU:359, one launch (start us, length us, event | category | flops | bytes accessed | tf_op | source)
XLA Modules:
  0.0 193.3 jit_solution(17598942953925067803)
XLA Ops:
  0.0 0.9 fusion.225
  0.9 3.1 %collective-permute-start = (bf16[4,16,512]{2,1,0:T(8,128)(2,1)S(1)}, bf16[4,16,512]{2,1,0:T(8,128)(2,1)S(1)}, u32[]{:S(2)}, u32[]{:S(2)}) collective-permute-start(bf16[4,16,512]{2,1,0:T(8,128)(2,1)S(1)} %get-tuple-element.51), channel_id=1, source_target_pairs={{0,64},{64,128},{128,192},{192,256},{256,320},{320,384},{384,448},... | collective-permute-start | bytes 196616 | tf_op jit(solution)/shard_map/ppermute | solution.py:15
  4.0 2.2 %collective-permute-start.1 = (bf16[4,16,512]{2,1,0:T(8,128)(2,1)S(1)}, bf16[4,16,512]{2,1,0:T(8,128)(2,1)S(1)}, u32[]{:S(2)}, u32[]{:S(2)}) collective-permute-start(bf16[4,16,512]{2,1,0:T(8,128)(2,1)S(1)} %get-tuple-element.52), channel_id=1, source_target_pairs={{64,0},{128,64},{192,128},{256,192},{320,256},{384,320},{448,384},... | collective-permute-start | bytes 196616 | tf_op jit(solution)/shard_map/ppermute | solution.py:18
  6.2 0.7 multiply_divide_fusion
  6.9 0.7 fusion.229
  7.6 0.7 multiply_divide_fusion.1
  8.2 0.7 fusion.227
  8.9 0.2 exponential_reduce_fusion
  9.1 0.7 fusion.228
  9.9 12.6 %multiply_exponential_fusion.32 = (f32[256,512]{1,0:T(8,128)S(1)}, f32[256,512]{1,0:T(8,128)S(1)}, pred[256,512]{1,0:T(8,128)(4,1)S(1)}, pred[256,512]{1,0:T(8,1...) fusion(f32[]{:T(128)} %bitcast.31, f32[]{:T(128)} %bitcast.30, ...), kind=kLoop, calls=%fused_computation.432 | loop fusion | flops 4325376 | bytes 3670080 | tf_op jit(solution)/shard_map/exp | solution.py:52
  22.5 0.0 copy-start.27
  22.5 1.1 multiply_exponential_fusion.31
  23.8 12.8 %multiply_exponential_fusion.33 = (f32[256,512]{1,0:T(8,128)}, f32[256,512]{1,0:T(8,128)S(1)}, pred[256,512]{1,0:T(8,128)(4,1)S(1)}, pred[256,512]{1,0:T(8,128)(...) fusion(f32[]{:T(128)} %bitcast.15, f32[]{:T(128)} %bitcast.14, ...), kind=kLoop, calls=%fused_computation.434 | loop fusion | flops 4325376 | bytes 3670080 | tf_op jit(solution)/shard_map/exp | solution.py:52
  36.6 3.4 %multiply_exponential_fusion.15 = (f32[256,512]{1,0:T(8,128)}, f32[256,512]{1,0:T(8,128)}, f32[256,512]{1,0:T(8,128)}, f32[256,512]{1,0:T(8,128)}, f32[256,512]{...) fusion(f32[256,512]{1,0:T(8,128)S(1)} %get-tuple-element.8), kind=kLoop, calls=%fused_computation.414 | loop fusion | flops 2097152 | bytes 8912896 | tf_op jit(solution)/shard_map/exp | solution.py:41
  40.1 11.0 %select_select_fusion.1 = f32[256,512]{1,0:T(8,128)S(1)} fusion(pred[256,512]{1,0:T(8,128)(4,1)S(1)} %get-tuple-element.42, pred[256,512]{1,0:T(8,128)(4,1)S(1)} %get-tuple-element.41, pred[256,512]{1,0:T(8,128)(4,1)S(1)} %get-tuple-element.40, pred[256,512]{1,0:T(8,128)(4,1)S(1)} %get-tuple-element.39, pred[256,512]{1,0:T(8,128)(4,1)S(1)} %get-tuple-element.38, ...), kind=kLoop, calls=%fused_computation.415 | loop fusion | flops 2097152 | bytes 2621504 | tf_op jit(solution)/shard_map/jit(_where)/select_n | solution.py:33
  51.1 0.0 copy-start.18
  51.1 0.0 collective-permute-done
  51.1 0.2 constant_dynamic-update-slice_fusion
  51.3 0.0 collective-permute-done.1
  51.5 9.1 %add_multiply_fusion.1 = f32[4,256,512]{2,1,0:T(8,128)S(1)} fusion(bf16[4,256,512]{2,1,0:T(8,128)(2,1)S(1)} %copy-done, bf16[4,272,512]{2,1,0:T(8,128)(2,1)S(1)} %constant_dynamic-update-slice_fusion.2, bf16[4,272,512]{2,1,0:T(8,128)(2,1)S(1)} %get-tuple-element.49, f32[256,512]{1,0:T(8,128)S(1)} %select_select_fusion.1, ...), kind=kLoop, calls=%fused_computation.347 | loop fusion | flops 51904512 | bytes 46137344 | tf_op jit(solution)/shard_map/mul | solution.py:45
  60.6 0.0 copy-done.18
  60.7 0.2 fusion.223
  60.9 3.1 %collective-permute-start.3 = (f32[4,256,16]{2,1,0:T(8,128)S(1)}, f32[4,256,16]{2,1,0:T(8,128)S(1)}, u32[]{:S(2)}, u32[]{:S(2)}) collective-permute-start(f32[4,256,16]{2,1,0:T(8,128)S(1)} %get-tuple-element.46), channel_id=1, source_target_pairs={{1,0},{2,1},{3,2},{4,3},{5,4},{6,5},{7,6},{8,7},{9,8},{10,9},{11,1... | collective-permute-start | bytes 196616 | tf_op jit(solution)/shard_map/ppermute | solution.py:18
  64.0 4.9 %collective-permute-start.2 = (f32[4,256,16]{2,1,0:T(8,128)S(1)}, f32[4,256,16]{2,1,0:T(8,128)}, u32[]{:S(2)}, u32[]{:S(2)}) collective-permute-start(f32[4,256,16]{2,1,0:T(8,128)S(1)} %get-tuple-element.45), channel_id=1, source_target_pairs={{0,1},{1,2},{2,3},{3,4},{4,5},{5,6},{6,7},{7,8},{8,9},{9,10},{10,1... | collective-permute-start | bytes 196616 | tf_op jit(solution)/shard_map/ppermute | solution.py:15
  68.9 0.7 fusion.226
  69.6 9.7 %collective-permute-done.3 = f32[4,256,16]{2,1,0:T(8,128)S(1)} collective-permute-done((f32[4,256,16]{2,1,0:T(8,128)S(1)}, f32[4,256,16]{2,1,0:T(8,128)S(1)}, u32[]{:S(2)}, u32[]{:S(2)}) %collective-permute-start.3) | collective-permute-done | bytes 65568 | tf_op jit(solution)/shard_map/ppermute | solution.py:18
  79.3 0.8 copy-done.28
  80.1 0.0 collective-permute-done.2
  80.1 30.3 %fusion.99 = bf16[4,256,512]{2,1,0:T(8,128)(2,1)S(1)} fusion(f32[4,256,512]{2,1,0:T(8,128)S(1)} %add_multiply_fusion.1, f32[4,256,16]{2,1,0:T(8,128)} %copy-done.28, f32[4,256,16]{2,1,0:T(8,128)} %collective-permute-done.2, f32[256,512]{1,0:T(8,128)} %copy-done.18, f32[256,512]{1,0:T(8,128)} %copy-done.17, f32[256,512]{1,0:T(8,128)} %copy-done.3, ...), kind=kLoop, calls=%fused_computation.249 | loop fusion | flops 51904512 | bytes 12713984 | tf_op jit(solution)/shard_map/convert_element_type | solution.py:63
  110.4 0.0 copy-start.19
  110.5 0.0 copy-start.21
  110.5 0.0 copy-start.23
  110.5 0.0 copy-start.24
  110.5 0.0 copy-start.25
  110.5 2.6 %collective-permute-start.5 = (bf16[4,16,512]{2,1,0:T(8,128)(2,1)S(1)}, bf16[4,16,512]{2,1,0:T(8,128)(2,1)S(1)}, u32[]{:S(2)}, u32[]{:S(2)}) collective-permute-start(bf16[4,16,512]{2,1,0:T(8,128)(2,1)S(1)} %get-tuple-element.48), channel_id=1, source_target_pairs={{64,0},{128,64},{192,128},{256,192},{320,256},{384,320},{448,384},... | collective-permute-start | bytes 196616 | tf_op jit(solution)/shard_map/ppermute | solution.py:18
  113.1 4.9 %collective-permute-start.4 = (bf16[4,16,512]{2,1,0:T(8,128)(2,1)S(1)}, bf16[4,16,512]{2,1,0:T(8,128)(2,1)S(1)}, u32[]{:S(2)}, u32[]{:S(2)}) collective-permute-start(bf16[4,16,512]{2,1,0:T(8,128)(2,1)S(1)} %get-tuple-element.47), channel_id=1, source_target_pairs={{0,64},{64,128},{128,192},{192,256},{256,320},{320,384},{384,448},... | collective-permute-start | bytes 196616 | tf_op jit(solution)/shard_map/ppermute | solution.py:15
  118.1 12.1 %select_select_fusion = f32[256,512]{1,0:T(8,128)S(1)} fusion(pred[256,512]{1,0:T(8,128)(4,1)} %get-tuple-element.24, pred[256,512]{1,0:T(8,128)(4,1)} %get-tuple-element.23, pred[256,512]{1,0:T(8,128)(4,1)} %get-tuple-element.22, pred[256,512]{1,0:T(8,128)(4,1)} %get-tuple-element.21, pred[256,512]{1,0:T(8,128)(4,1)} %get-tuple-element.20, ...), kind=kLoop, calls=%fused_computation.398 | loop fusion | flops 2097152 | bytes 2621504 | tf_op jit(solution)/shard_map/jit(_where)/select_n | solution.py:33
  130.2 0.0 collective-permute-done.5
  130.2 0.0 collective-permute-done.4
  130.2 0.0 copy-done.19
  130.2 11.8 %add_multiply_fusion = f32[4,256,512]{2,1,0:T(8,128)S(1)} fusion(bf16[4,256,512]{2,1,0:T(8,128)(2,1)S(1)} %fusion.99, bf16[4,16,512]{2,1,0:T(8,128)(2,1)S(1)} %collective-permute-done.5, bf16[4,16,512]{2,1,0:T(8,128)(2,1)S(1)} %collective-permute-done.4, f32[256,512]{1,0:T(8,128)S(1)} %select_select_fusion, f32[256,512]{1,0:T(8,128)} %get-tuple-element.68, ...), kind=kLoop, calls=%fused_computation.346 | loop fusion | flops 102236160 | bytes 12713984 | tf_op jit(solution)/shard_map/mul | solution.py:45
  142.1 0.2 fusion.222
  142.3 2.1 %collective-permute-start.7 = (f32[4,256,16]{2,1,0:T(8,128)S(1)}, f32[4,256,16]{2,1,0:T(8,128)S(1)}, u32[]{:S(2)}, u32[]{:S(2)}) collective-permute-start(f32[4,256,16]{2,1,0:T(8,128)S(1)} %get-tuple-element.44), channel_id=1, source_target_pairs={{1,0},{2,1},{3,2},{4,3},{5,4},{6,5},{7,6},{8,7},{9,8},{10,9},{11,1... | collective-permute-start | bytes 196616 | tf_op jit(solution)/shard_map/ppermute | solution.py:18
  144.4 6.5 %collective-permute-start.6 = (f32[4,256,16]{2,1,0:T(8,128)S(1)}, f32[4,256,16]{2,1,0:T(8,128)}, u32[]{:S(2)}, u32[]{:S(2)}) collective-permute-start(f32[4,256,16]{2,1,0:T(8,128)S(1)} %get-tuple-element.43), channel_id=1, source_target_pairs={{0,1},{1,2},{2,3},{3,4},{4,5},{5,6},{6,7},{7,8},{8,9},{9,10},{10,1... | collective-permute-start | bytes 196616 | tf_op jit(solution)/shard_map/ppermute | solution.py:15
  150.9 10.5 %collective-permute-done.7 = f32[4,256,16]{2,1,0:T(8,128)S(1)} collective-permute-done((f32[4,256,16]{2,1,0:T(8,128)S(1)}, f32[4,256,16]{2,1,0:T(8,128)S(1)}, u32[]{:S(2)}, u32[]{:S(2)}) %collective-permute-start.7) | collective-permute-done | bytes 65568 | tf_op jit(solution)/shard_map/ppermute | solution.py:18
  161.4 0.8 copy-done.29
  162.2 0.0 collective-permute-done.6
  162.2 30.9 %fusion.5 = bf16[4,256,512]{2,1,0:T(8,128)(2,1)} fusion(f32[4,256,512]{2,1,0:T(8,128)S(1)} %add_multiply_fusion, f32[4,256,16]{2,1,0:T(8,128)} %copy-done.29, f32[4,256,16]{2,1,0:T(8,128)} %collective-permute-done.6, f32[256,512]{1,0:T(8,128)} %copy-done.26, f32[256,512]{1,0:T(8,128)} %get-tuple-element.68, f32[256,512]{1,0:T(8,128)} %get-tuple-element.54, ...), kind=kLoop, calls=%fused_computation.155 | loop fusion | flops 51904512 | bytes 12713984 | tf_op jit(solution)/shard_map/convert_element_type | solution.py:63
  (54 shorter events, 0.1 us)
Async XLA Ops:
  0.9 50.2 %collective-permute-start = (bf16[4,16,512]{2,1,0:T(8,128)(2,1)S(1)}, bf16[4,16,512]{2,1,0:T(8,128)(2,1)S(1)}, u32[]{:S(2)}, u32[]{:S(2)}) collective-permute-start(bf16[4,16,512]{2,1,0:T(8,128)(2,1)S(1)} %get-tuple-element.51), channel_id=1, source_target_pairs={{0,64},{64,128},{128,192},{192,256},{256,320},{320,384},{384,448},... | collective-permute-start | bytes 196616 | tf_op jit(solution)/shard_map/ppermute | solution.py:15
  4.0 47.3 %collective-permute-start.1 = (bf16[4,16,512]{2,1,0:T(8,128)(2,1)S(1)}, bf16[4,16,512]{2,1,0:T(8,128)(2,1)S(1)}, u32[]{:S(2)}, u32[]{:S(2)}) collective-permute-start(bf16[4,16,512]{2,1,0:T(8,128)(2,1)S(1)} %get-tuple-element.52), channel_id=1, source_target_pairs={{64,0},{128,64},{192,128},{256,192},{320,256},{384,320},{448,384},... | collective-permute-start | bytes 196616 | tf_op jit(solution)/shard_map/ppermute | solution.py:18
  22.5 28.8 %copy-start.1 = (f32[256,512]{1,0:T(8,128)}, f32[256,512]{1,0:T(8,128)S(1)}, u32[]{:S(2)}) copy-start(f32[256,512]{1,0:T(8,128)S(1)} %get-tuple-element.25) | copy-start | bytes 1572868
  22.5 1.3 copy-start.27
  23.6 27.7 %copy-start.2 = (f32[256,512]{1,0:T(8,128)}, f32[256,512]{1,0:T(8,128)S(1)}, u32[]{:S(2)}) copy-start(f32[256,512]{1,0:T(8,128)S(1)} %get-tuple-element.69) | copy-start | bytes 1572868
  23.6 27.7 %copy-start.3 = (f32[256,512]{1,0:T(8,128)}, f32[256,512]{1,0:T(8,128)S(1)}, u32[]{:S(2)}) copy-start(f32[256,512]{1,0:T(8,128)S(1)} %get-tuple-element.70) | copy-start | bytes 1572868
  23.6 27.7 %copy-start.4 = (f32[256,512]{1,0:T(8,128)}, f32[256,512]{1,0:T(8,128)S(1)}, u32[]{:S(2)}) copy-start(f32[256,512]{1,0:T(8,128)S(1)} %get-tuple-element.71) | copy-start | bytes 1572868
  23.7 27.7 %copy-start.5 = (f32[256,512]{1,0:T(8,128)}, f32[256,512]{1,0:T(8,128)S(1)}, u32[]{:S(2)}) copy-start(f32[256,512]{1,0:T(8,128)S(1)} %get-tuple-element.72) | copy-start | bytes 1572868
  23.7 27.7 %copy-start.6 = (f32[256,512]{1,0:T(8,128)}, f32[256,512]{1,0:T(8,128)S(1)}, u32[]{:S(2)}) copy-start(f32[256,512]{1,0:T(8,128)S(1)} %get-tuple-element.73) | copy-start | bytes 1572868
  23.7 27.7 %copy-start.7 = (f32[256,512]{1,0:T(8,128)}, f32[256,512]{1,0:T(8,128)S(1)}, u32[]{:S(2)}) copy-start(f32[256,512]{1,0:T(8,128)S(1)} %get-tuple-element.74) | copy-start | bytes 1572868
  23.7 27.7 %copy-start.8 = (f32[256,512]{1,0:T(8,128)}, f32[256,512]{1,0:T(8,128)S(1)}, u32[]{:S(2)}) copy-start(f32[256,512]{1,0:T(8,128)S(1)} %get-tuple-element.75) | copy-start | bytes 1572868
  23.7 27.7 %copy-start.9 = (f32[256,512]{1,0:T(8,128)}, f32[256,512]{1,0:T(8,128)S(1)}, u32[]{:S(2)}) copy-start(f32[256,512]{1,0:T(8,128)S(1)} %get-tuple-element.76) | copy-start | bytes 1572868
  23.7 27.7 %copy-start.10 = (f32[256,512]{1,0:T(8,128)}, f32[256,512]{1,0:T(8,128)S(1)}, u32[]{:S(2)}) copy-start(f32[256,512]{1,0:T(8,128)S(1)} %get-tuple-element.77) | copy-start | bytes 1572868
  23.7 27.7 %copy-start.11 = (f32[256,512]{1,0:T(8,128)}, f32[256,512]{1,0:T(8,128)S(1)}, u32[]{:S(2)}) copy-start(f32[256,512]{1,0:T(8,128)S(1)} %get-tuple-element.78) | copy-start | bytes 1572868
  23.7 27.7 %copy-start.12 = (f32[256,512]{1,0:T(8,128)}, f32[256,512]{1,0:T(8,128)S(1)}, u32[]{:S(2)}) copy-start(f32[256,512]{1,0:T(8,128)S(1)} %get-tuple-element.79) | copy-start | bytes 1572868
  23.7 27.7 %copy-start.13 = (f32[256,512]{1,0:T(8,128)}, f32[256,512]{1,0:T(8,128)S(1)}, u32[]{:S(2)}) copy-start(f32[256,512]{1,0:T(8,128)S(1)} %get-tuple-element.80) | copy-start | bytes 1572868
  23.8 27.7 %copy-start.14 = (f32[256,512]{1,0:T(8,128)}, f32[256,512]{1,0:T(8,128)S(1)}, u32[]{:S(2)}) copy-start(f32[256,512]{1,0:T(8,128)S(1)} %get-tuple-element.81) | copy-start | bytes 1572868
  23.8 27.7 %copy-start.15 = (f32[256,512]{1,0:T(8,128)}, f32[256,512]{1,0:T(8,128)S(1)}, u32[]{:S(2)}) copy-start(f32[256,512]{1,0:T(8,128)S(1)} %get-tuple-element.82) | copy-start | bytes 1572868
  23.8 27.7 %copy-start.16 = (f32[256,512]{1,0:T(8,128)}, f32[256,512]{1,0:T(8,128)S(1)}, u32[]{:S(2)}) copy-start(f32[256,512]{1,0:T(8,128)S(1)} %get-tuple-element.83) | copy-start | bytes 1572868
  23.8 27.7 %copy-start.17 = (f32[256,512]{1,0:T(8,128)}, f32[256,512]{1,0:T(8,128)S(1)}, u32[]{:S(2)}) copy-start(f32[256,512]{1,0:T(8,128)S(1)} %get-tuple-element.84) | copy-start | bytes 1572868
  40.1 11.0 %copy-start = (bf16[4,256,512]{2,1,0:T(8,128)(2,1)S(1)}, bf16[4,256,512]{2,1,0:T(8,128)(2,1)}, u32[]{:S(2)}) copy-start(bf16[4,256,512]{2,1,0:T(8,128)(2,1)} %param.5) | copy-start | bytes 3145732
  51.1 9.6 %copy-start.18 = (f32[256,512]{1,0:T(8,128)}, f32[256,512]{1,0:T(8,128)S(1)}, u32[]{:S(2)}) copy-start(f32[256,512]{1,0:T(8,128)S(1)} %select_select_fusion.1) | copy-start | bytes 1572868
  60.9 18.4 %collective-permute-start.3 = (f32[4,256,16]{2,1,0:T(8,128)S(1)}, f32[4,256,16]{2,1,0:T(8,128)S(1)}, u32[]{:S(2)}, u32[]{:S(2)}) collective-permute-start(f32[4,256,16]{2,1,0:T(8,128)S(1)} %get-tuple-element.46), channel_id=1, source_target_pairs={{1,0},{2,1},{3,2},{4,3},{5,4},{6,5},{7,6},{8,7},{9,8},{10,9},{11,1... | collective-permute-start | bytes 196616 | tf_op jit(solution)/shard_map/ppermute | solution.py:18
  64.0 16.1 %collective-permute-start.2 = (f32[4,256,16]{2,1,0:T(8,128)S(1)}, f32[4,256,16]{2,1,0:T(8,128)}, u32[]{:S(2)}, u32[]{:S(2)}) collective-permute-start(f32[4,256,16]{2,1,0:T(8,128)S(1)} %get-tuple-element.45), channel_id=1, source_target_pairs={{0,1},{1,2},{2,3},{3,4},{4,5},{5,6},{6,7},{7,8},{8,9},{9,10},{10,1... | collective-permute-start | bytes 196616 | tf_op jit(solution)/shard_map/ppermute | solution.py:15
  79.3 0.8 copy-start.28
  110.4 19.8 %copy-start.19 = (f32[256,512]{1,0:T(8,128)S(1)}, f32[256,512]{1,0:T(8,128)}, u32[]{:S(2)}) copy-start(f32[256,512]{1,0:T(8,128)} %get-tuple-element.7) | copy-start | bytes 1572868
  110.5 19.8 %copy-start.21 = (f32[256,512]{1,0:T(8,128)S(1)}, f32[256,512]{1,0:T(8,128)}, u32[]{:S(2)}) copy-start(f32[256,512]{1,0:T(8,128)} %get-tuple-element.53) | copy-start | bytes 1572868
  110.5 19.8 %copy-start.23 = (f32[256,512]{1,0:T(8,128)S(1)}, f32[256,512]{1,0:T(8,128)}, u32[]{:S(2)}) copy-start(f32[256,512]{1,0:T(8,128)} %get-tuple-element.54) | copy-start | bytes 1572868
  110.5 19.8 %copy-start.24 = (f32[256,512]{1,0:T(8,128)S(1)}, f32[256,512]{1,0:T(8,128)}, u32[]{:S(2)}) copy-start(f32[256,512]{1,0:T(8,128)} %get-tuple-element.55) | copy-start | bytes 1572868
  110.5 19.8 %copy-start.25 = (f32[256,512]{1,0:T(8,128)S(1)}, f32[256,512]{1,0:T(8,128)}, u32[]{:S(2)}) copy-start(f32[256,512]{1,0:T(8,128)} %get-tuple-element.56) | copy-start | bytes 1572868
  110.5 19.7 %collective-permute-start.5 = (bf16[4,16,512]{2,1,0:T(8,128)(2,1)S(1)}, bf16[4,16,512]{2,1,0:T(8,128)(2,1)S(1)}, u32[]{:S(2)}, u32[]{:S(2)}) collective-permute-start(bf16[4,16,512]{2,1,0:T(8,128)(2,1)S(1)} %get-tuple-element.48), channel_id=1, source_target_pairs={{64,0},{128,64},{192,128},{256,192},{320,256},{384,320},{448,384},... | collective-permute-start | bytes 196616 | tf_op jit(solution)/shard_map/ppermute | solution.py:18
  113.1 17.1 %collective-permute-start.4 = (bf16[4,16,512]{2,1,0:T(8,128)(2,1)S(1)}, bf16[4,16,512]{2,1,0:T(8,128)(2,1)S(1)}, u32[]{:S(2)}, u32[]{:S(2)}) collective-permute-start(bf16[4,16,512]{2,1,0:T(8,128)(2,1)S(1)} %get-tuple-element.47), channel_id=1, source_target_pairs={{0,64},{64,128},{128,192},{192,256},{256,320},{320,384},{384,448},... | collective-permute-start | bytes 196616 | tf_op jit(solution)/shard_map/ppermute | solution.py:15
  130.2 11.9 %copy-start.26 = (f32[256,512]{1,0:T(8,128)}, f32[256,512]{1,0:T(8,128)S(1)}, u32[]{:S(2)}) copy-start(f32[256,512]{1,0:T(8,128)S(1)} %select_select_fusion) | copy-start | bytes 1572868
  142.0 20.2 %copy-start.20 = (f32[256,512]{1,0:T(8,128)S(1)}, f32[256,512]{1,0:T(8,128)}, u32[]{:S(2)}) copy-start(f32[256,512]{1,0:T(8,128)} %get-tuple-element.7) | copy-start | bytes 1572868
  142.0 20.2 %copy-start.22 = (f32[256,512]{1,0:T(8,128)S(1)}, f32[256,512]{1,0:T(8,128)}, u32[]{:S(2)}) copy-start(f32[256,512]{1,0:T(8,128)} %get-tuple-element.53) | copy-start | bytes 1572868
  142.3 19.2 %collective-permute-start.7 = (f32[4,256,16]{2,1,0:T(8,128)S(1)}, f32[4,256,16]{2,1,0:T(8,128)S(1)}, u32[]{:S(2)}, u32[]{:S(2)}) collective-permute-start(f32[4,256,16]{2,1,0:T(8,128)S(1)} %get-tuple-element.44), channel_id=1, source_target_pairs={{1,0},{2,1},{3,2},{4,3},{5,4},{6,5},{7,6},{8,7},{9,8},{10,9},{11,1... | collective-permute-start | bytes 196616 | tf_op jit(solution)/shard_map/ppermute | solution.py:18
  144.4 17.8 %collective-permute-start.6 = (f32[4,256,16]{2,1,0:T(8,128)S(1)}, f32[4,256,16]{2,1,0:T(8,128)}, u32[]{:S(2)}, u32[]{:S(2)}) collective-permute-start(f32[4,256,16]{2,1,0:T(8,128)S(1)} %get-tuple-element.43), channel_id=1, source_target_pairs={{0,1},{1,2},{2,3},{3,4},{4,5},{5,6},{6,7},{7,8},{8,9},{9,10},{10,1... | collective-permute-start | bytes 196616 | tf_op jit(solution)/shard_map/ppermute | solution.py:15
  161.4 0.8 copy-start.29
where the time goes:
time: 194 us; the launch traced here: 193 us
  other arithmetic  137 us (71%)
  starting transfers between devices  29.5 us (15%)
  waiting for transfers between devices  20.2 us (10%)
  local copies, waits for them, and re-layouts  6.05 us (3%)
    convert_element_type x2, other arithmetic, smooth(): return result.astype(jnp.bfloat16)  61.2 us
    exp x2, other arithmetic, cols_pass(): weight = jnp.exp(-float(offset * offset) * spread)  25.5 us
    select_n x2, other arithmetic, class_weights(): scale_cell = jnp.where(hit, scale_tab[number], scale_cell)  23.1 us
    mul x2, other arithmetic, rows_pass(): return accum * scale_cell[None]  20.9 us
    ppermute x4, waiting for transfers between devices, extended(): lax.ppermute(lax.slice_in_dim(block, 0, width, axis=dim), axis, backward)  20.2 us
    ppermute x4, starting transfers between devices, extended(): lax.ppermute(lax.slice_in_dim(block, block.shape[dim] - width, None, axis...  19.4 us
    ppermute x4, starting transfers between devices, extended(): lax.ppermute(lax.slice_in_dim(block, 0, width, axis=dim), axis, backward)  10 us
    exp x2, other arithmetic, rows_pass(): weight = jnp.exp(-float(offset * offset) * spread)  4.51 us
  transfers between devices with their start and end apart: 8, of which 2 were waited for; matrix products, arithmetic and copies ran while one was open for 30% of the time, Pallas kernels for 0%

commit v1 on v0

v1 whole, which is shorter than its diff:
```python
import jax
import jax.numpy as jnp
from jax import lax
from jax.experimental import pallas as pl
from jax.experimental.pallas import tpu as pltpu
from jax.sharding import PartitionSpec as P

RADIUS = 16
NCLASS = 16
BANDS = 4
ROWS = 256
COLS = 512
LANES = 128
COLBLK = COLS // LANES
ROWBLK = ROWS // LANES
WIDE = 2 * RADIUS
TALL = ROWS + 2 * RADIUS
FULL = ROWS + 2 * WIDE
BROAD = COLS + 2 * RADIUS
CODES = TALL // 2


def lookup(table, codes):
    return jnp.take_along_axis(jnp.broadcast_to(table, codes.shape), codes, axis=1)


def weighted(sources, q, scale):
    square = q * q
    weight = q
    ratio = q * square
    totals = [source(0) for source in sources]
    for k in range(1, RADIUS + 1):
        if k > 1:
            weight = weight * ratio
            ratio = ratio * square
        totals = [
            total + weight * (source(k) + source(-k)) for total, source in zip(totals, sources)
        ]
    return [total * scale for total in totals]


def smooth_blocks(source_ref, blocks, lead, code_ref, code_block, q_tab, s_tab, out_ref, length, rounded=False):
    def tile(step, _):
        start = pl.multiple_of(step * 8, 8)
        codes = code_ref[code_block, pl.ds(start, 8), :]
        q = lookup(q_tab, codes)
        scale = lookup(s_tab, codes)

        def reader(block):
            return lambda k: source_ref[block, pl.ds(start + lead + k, 8), :]

        results = weighted([reader(block) for block in blocks], q, scale)
        for block, result in zip(blocks, results):
            if rounded:
                result = result.astype(jnp.bfloat16).astype(jnp.float32)
            out_ref[block, pl.ds(start, 8), :] = result
        return 0

    lax.fori_loop(0, length // 8, tile, 0, unroll=2)


def kernel(
    tables_ref, heights_ref, low_ref, high_ref, left_ref, right_ref, sigma_ref, window_ref, out_ref,
    rows_in, rows_out, cols_in, cols_out, sig_row, sig_col, win_row, win_col,
):
    q_sig = tables_ref[0:1, :]
    s_sig = tables_ref[1:2, :]
    q_win = tables_ref[2:3, :]
    s_win = tables_ref[3:4, :]

    for b in range(BANDS):
        for j in range(COLBLK):
            lanes = slice(j * LANES, (j + 1) * LANES)
            block = b * COLBLK + j
            rows_in[block, 0:WIDE, :] = low_ref[b * WIDE:(b + 1) * WIDE, lanes].astype(jnp.float32)
            rows_in[block, WIDE:WIDE + ROWS, :] = heights_ref[b, :, lanes].astype(jnp.float32)
            rows_in[block, WIDE + ROWS:FULL, :] = high_ref[b * WIDE:(b + 1) * WIDE, lanes].astype(jnp.float32)
    rows_in[16, :, :] = left_ref[0:FULL, :].astype(jnp.float32)
    rows_in[17, :, :] = right_ref[0:FULL, :].astype(jnp.float32)

    for j in range(COLBLK):
        lanes = slice(j * LANES, (j + 1) * LANES)
        edge = slice(BANDS * WIDE, BANDS * WIDE + RADIUS)
        sig_row[j, 0:RADIUS, :] = low_ref[edge, lanes].astype(jnp.float32).astype(jnp.int32)
        sig_row[j, RADIUS:RADIUS + ROWS, :] = sigma_ref[:, lanes] + 1
        sig_row[j, RADIUS + ROWS:TALL, :] = high_ref[edge, lanes].astype(jnp.float32).astype(jnp.int32)
        win_row[j, :, :] = window_ref[:, lanes] + 1
    halves = []
    for side, ref in ((4, left_ref), (5, right_ref)):
        packed = ref[FULL:FULL + CODES, :].astype(jnp.float32).astype(jnp.int32)
        for half in range(2):
            piece = packed[:, half * WIDE:(half + 1) * WIDE]
            sig_row[side, half * CODES:(half + 1) * CODES, :] = jnp.concatenate([piece] * BANDS, axis=1)
        halves.append([packed[0:LANES, 2 * WIDE + h * RADIUS:2 * WIDE + (h + 1) * RADIUS] for h in range(2)])
    for half in range(2):
        pair = [halves[0][half], halves[1][half]]
        win_row[4, half * LANES:(half + 1) * LANES, :] = jnp.concatenate(pair * BANDS, axis=1)

    for j in range(COLBLK):
        for i in range(ROWBLK):
            body = sig_row[j, RADIUS + i * LANES:RADIUS + (i + 1) * LANES, :]
            sig_col[i, RADIUS + j * LANES:RADIUS + (j + 1) * LANES, :] = body.T
            win_col[i, j * LANES:(j + 1) * LANES, :] = win_row[j, i * LANES:(i + 1) * LANES, :].T
        edges = jnp.concatenate([sig_row[j, 0:RADIUS, :], sig_row[j, RADIUS + ROWS:TALL, :]] * BANDS, axis=0)
        sig_col[2, RADIUS + j * LANES:RADIUS + (j + 1) * LANES, :] = edges.T
    for side, block in enumerate((4, 5)):
        inner = slice(RADIUS, WIDE) if side == 0 else slice(0, RADIUS)
        place = slice(0, RADIUS) if side == 0 else slice(RADIUS + COLS, BROAD)
        for i in range(ROWBLK):
            body = sig_row[block, RADIUS + i * LANES:RADIUS + (i + 1) * LANES, :].T
            sig_col[i, place, :] = body[inner, :]
        edges = jnp.concatenate([sig_row[block, 0:RADIUS, :], sig_row[block, RADIUS + ROWS:TALL, :]] * BANDS, axis=0)
        sig_col[2, place, :] = edges.T[inner, :]

    for j in range(COLBLK):
        blocks = [b * COLBLK + j for b in range(BANDS)]
        smooth_blocks(rows_in, blocks, RADIUS, sig_row, j, q_sig, s_sig, rows_out, TALL)
    for side in range(2):
        smooth_blocks(rows_in, [16 + side], RADIUS, sig_row, 4 + side, q_sig, s_sig, rows_out, TALL)

    for j in range(COLBLK):
        place = slice(WIDE + j * LANES, WIDE + (j + 1) * LANES)
        for b in range(BANDS):
            for i in range(ROWBLK):
                body = rows_out[b * COLBLK + j, RADIUS + i * LANES:RADIUS + (i + 1) * LANES, :]
                cols_in[b * ROWBLK + i, place, :] = body.T
        edges = []
        for b in range(BANDS):
            edges += [rows_out[b * COLBLK + j, 0:RADIUS, :], rows_out[b * COLBLK + j, RADIUS + ROWS:TALL, :]]
        cols_in[8, place, :] = jnp.concatenate(edges, axis=0).T
    for side in range(2):
        place = slice(0, WIDE) if side == 0 else slice(WIDE + COLS, 2 * WIDE + COLS)
        for i in range(ROWBLK):
            body = rows_out[16 + side, RADIUS + i * LANES:RADIUS + (i + 1) * LANES, :].T
            for b in range(BANDS):
                cols_in[b * ROWBLK + i, place, :] = body[b * WIDE:(b + 1) * WIDE, :]
        top = rows_out[16 + side, 0:RADIUS, :]
        bottom = rows_out[16 + side, RADIUS + ROWS:TALL, :]
        edges = jnp.concatenate([top, bottom] * BANDS, axis=0).T
        lane = lax.broadcasted_iota(jnp.int32, (WIDE, LANES), 1) // WIDE
        merged = edges[0:WIDE, :]
        for b in range(1, BANDS):
            merged = jnp.where(lane == b, edges[b * WIDE:(b + 1) * WIDE, :], merged)
        cols_in[8, place, :] = merged

    for i in range(ROWBLK):
        blocks = [b * ROWBLK + i for b in range(BANDS)]
        smooth_blocks(cols_in, blocks, RADIUS, sig_col, i, q_sig, s_sig, cols_out, BROAD, True)
    smooth_blocks(cols_in, [8], RADIUS, sig_col, 2, q_sig, s_sig, cols_out, BROAD, True)

    for j in range(COLBLK):
        place = slice(RADIUS + j * LANES, RADIUS + (j + 1) * LANES)
        for b in range(BANDS):
            for i in range(ROWBLK):
                rows_in[b * COLBLK + j, RADIUS + i * LANES:RADIUS + (i + 1) * LANES, :] = cols_out[b * ROWBLK + i, place, :].T
        edges = cols_out[8, place, :].T
        for b in range(BANDS):
            rows_in[b * COLBLK + j, 0:RADIUS, :] = edges[b * WIDE:b * WIDE + RADIUS, :]
            rows_in[b * COLBLK + j, RADIUS + ROWS:TALL, :] = edges[b * WIDE + RADIUS:(b + 1) * WIDE, :]
    for i in range(ROWBLK):
        edges = []
        for b in range(BANDS):
            edges += [cols_out[b * ROWBLK + i, 0:RADIUS, :], cols_out[b * ROWBLK + i, RADIUS + COLS:BROAD, :]]
        rows_in[16, RADIUS + i * LANES:RADIUS + (i + 1) * LANES, :] = jnp.concatenate(edges, axis=0).T
    both = jnp.concatenate([cols_out[8, 0:RADIUS, :], cols_out[8, RADIUS + COLS:BROAD, :]] * BANDS, axis=0).T
    lane = lax.broadcasted_iota(jnp.int32, (WIDE, LANES), 1) // WIDE
    merged = both[0:WIDE, :]
    for b in range(1, BANDS):
        merged = jnp.where(lane == b, both[b * WIDE:(b + 1) * WIDE, :], merged)
    rows_in[16, 0:RADIUS, :] = merged[0:RADIUS, :]
    rows_in[16, RADIUS + ROWS:TALL, :] = merged[RADIUS:WIDE, :]

    for j in range(COLBLK):
        blocks = [b * COLBLK + j for b in range(BANDS)]
        smooth_blocks(rows_in, blocks, RADIUS, win_row, j, q_win, s_win, rows_out, ROWS)
    smooth_blocks(rows_in, [16], RADIUS, win_row, 4, q_win, s_win, rows_out, ROWS)

    for i in range(ROWBLK):
        for j in range(COLBLK):
            for b in range(BANDS):
                body = rows_out[b * COLBLK + j, i * LANES:(i + 1) * LANES, :]
                cols_in[b * ROWBLK + i, RADIUS + j * LANES:RADIUS + (j + 1) * LANES, :] = body.T
        body = rows_out[16, i * LANES:(i + 1) * LANES, :].T
        for b in range(BANDS):
            cols_in[b * ROWBLK + i, 0:RADIUS, :] = body[b * WIDE:b * WIDE + RADIUS, :]
            cols_in[b * ROWBLK + i, RADIUS + COLS:BROAD, :] = body[b * WIDE + RADIUS:(b + 1) * WIDE, :]

    for i in range(ROWBLK):
        blocks = [b * ROWBLK + i for b in range(BANDS)]
        smooth_blocks(cols_in, blocks, RADIUS, win_col, i, q_win, s_win, cols_out, COLS)

    for b in range(BANDS):
        for i in range(ROWBLK):
            for j in range(COLBLK):
                body = cols_out[b * ROWBLK + i, j * LANES:(j + 1) * LANES, :].T
                out_ref[b, i * LANES:(i + 1) * LANES, j * LANES:(j + 1) * LANES] = body.astype(jnp.bfloat16)


def class_tables(table):
    spread = 0.5 / (table * table)
    offsets = jnp.arange(-RADIUS, RADIUS + 1).astype(jnp.float32)
    norm = jnp.sum(jnp.exp(-(offsets * offsets)[None, :] * spread[:, None]), axis=1)
    return jnp.pad(jnp.stack([jnp.exp(-spread), 1.0 / norm]), ((0, 0), (1, LANES - NCLASS - 1)))


def exchange(low_edge, high_edge, axis):
    count = lax.axis_size(axis)
    forward = [(i, i + 1) for i in range(count - 1)]
    backward = [(target, source) for source, target in forward]
    return lax.ppermute(high_edge, axis, forward), lax.ppermute(low_edge, axis, backward)


def per_device(heights, sigma_class, window_class, sigma_table, window_table):
    tables = jnp.concatenate([class_tables(sigma_table), class_tables(window_table)], axis=0)
    tables = jnp.pad(tables, ((0, 4), (0, 0)))
    sigma_code = (sigma_class + 1).astype(jnp.bfloat16)
    window_code = (window_class + 1).astype(jnp.bfloat16)

    def row_edge(start, code_start):
        band_rows = heights[:, start:start + WIDE, :].reshape(BANDS * WIDE, COLS)
        return jnp.concatenate([band_rows, sigma_code[code_start:code_start + RADIUS]], axis=0)

    low, high = exchange(row_edge(0, 0), row_edge(ROWS - WIDE, ROWS - RADIUS), "lat")

    def column_edge(start, inner):
        cols = slice(start, start + WIDE)
        low_rows = low[:BANDS * WIDE, cols].reshape(BANDS, WIDE, WIDE)
        high_rows = high[:BANDS * WIDE, cols].reshape(BANDS, WIDE, WIDE)
        tall = jnp.concatenate([low_rows, heights[:, :, cols], high_rows], axis=1)
        tall = jnp.transpose(tall, (1, 0, 2)).reshape(FULL, BANDS * WIDE)
        code = jnp.concatenate([low[BANDS * WIDE:, cols], sigma_code[:, cols], high[BANDS * WIDE:, cols]], axis=0)
        near = jnp.pad(window_code[:, inner:inner + RADIUS].reshape(2, LANES, RADIUS), ((0, 0), (0, CODES - LANES), (0, 0)))
        pad = jnp.zeros((CODES, LANES - 3 * WIDE), jnp.bfloat16)
        packed = jnp.concatenate([code[:CODES], code[CODES:], near[0], near[1], pad], axis=1)
        return jnp.concatenate([tall, packed], axis=0)

    left, right = exchange(column_edge(0, 0), column_edge(COLS - WIDE, COLS - RADIUS), "lon")

    vmem = pl.BlockSpec(memory_space=pltpu.VMEM)
    return pl.pallas_call(
        kernel,
        out_shape=jax.ShapeDtypeStruct((BANDS, ROWS, COLS), jnp.bfloat16),
        in_specs=[vmem] * 8,
        out_specs=vmem,
        scratch_shapes=[
            pltpu.VMEM((18, FULL, LANES), jnp.float32),
            pltpu.VMEM((18, TALL, LANES), jnp.float32),
            pltpu.VMEM((9, COLS + 2 * WIDE, LANES), jnp.float32),
            pltpu.VMEM((9, BROAD, LANES), jnp.float32),
            pltpu.VMEM((6, TALL, LANES), jnp.int32),
            pltpu.VMEM((3, BROAD, LANES), jnp.int32),
            pltpu.VMEM((5, ROWS, LANES), jnp.int32),
            pltpu.VMEM((2, COLS, LANES), jnp.int32),
        ],
        name="smooth",
    )(tables, heights, low, high, left, right, sigma_class, window_class)


def solution(mesh):
    placed = (P(None, "lat", "lon"), P("lat", "lon"), P("lat", "lon"), P(), P())
    return jax.shard_map(
        per_device, mesh=mesh, in_specs=placed, out_specs=P(None, "lat", "lon"), check_vma=False
    )
```

time: 194 us -> 79.7 us (0.41)
  the two profiles are of different devices: /device:TPU:359 before, /device:TPU:247 now
where the time goes in v1:
time: 79.7 us; the launch traced here: 79.5 us
  Pallas kernels  47.7 us (60%)
  starting transfers between devices  13.7 us (17%)
  waiting for transfers between devices  10.7 us (13%)
  local copies, waits for them, and re-layouts  4.61 us (6%)
  other arithmetic  2.49 us (3%)
    pallas_call x1, Pallas kernels, per_device(): pl.pallas_call(kernel, out_shape=jax.ShapeDtypeStruct((BANDS, ROWS, COLS)...  47.7 us
    ppermute x2, waiting for transfers between devices, exchange(): lax.ppermute(low_edge, axis, backward)  10.7 us
    ppermute x2, starting transfers between devices, exchange(): lax.ppermute(high_edge, axis, forward)  9.34 us
    ppermute x2, starting transfers between devices, exchange(): lax.ppermute(low_edge, axis, backward)  4.38 us
    unnamed x18, local copies, waits for them, and re-layouts  2.06 us
  transfers between devices with their start and end apart: 4, of which 2 were waited for; matrix products, arithmetic and copies ran while one was open for 3% of the time, Pallas kernels for 0%

profile of v1, /device:TPU:247, one launch (start us, length us, event | category | flops | bytes accessed | tf_op | source)
XLA Modules:
  0.0 79.5 jit_solution(8425827059586893427)
XLA Ops:
  0.0 0.0 copy-start
  0.0 1.2 %add_convert_fusion.1 = bf16[256,512]{1,0:T(8,128)(2,1)S(1)} fusion(s32[256,512]{1,0:T(8,128)} %sigma_ref.1), kind=kLoop, calls=%fused_computation.1 | loop fusion | flops 262144 | bytes 786432 | tf_op jit(solution)/shard_map/convert_element_type | solution.py:216
  1.2 1.0 %fusion.5 = (bf16[4,32,512]{2,1,0:T(8,128)(2,1)S(1)}, bf16[4,32,512]{2,1,0:T(8,128)(2,1)S(1)}) fusion(bf16[4,256,512]{2,1,0:T(8,128)(2,1)} %heights_ref.1), kind=kLoop, calls=%fused_computation.35 | loop fusion | bytes 524288 | tf_op jit(solution)/shard_map/slice | solution.py:220
  2.2 2.8 %collective-permute-start = (bf16[144,512]{1,0:T(8,128)(2,1)S(1)}, bf16[144,512]{1,0:T(8,128)(2,1)S(1)}, u32[]{:S(2)}, u32[]{:S(2)}) collective-permute-start(bf16[144,512]{1,0:T(8,128)(2,1)S(1)} %pad_maximum_fusion), channel_id=1, source_target_pairs={{0,64},{64,128},{128,192},{192,256},{256,320},{320,384},{384,448},... | collective-permute-start | bytes 442376 | tf_op jit(solution)/shard_map/ppermute | solution.py:210
  5.1 2.5 %collective-permute-start.1 = (bf16[144,512]{1,0:T(8,128)(2,1)S(1)}, bf16[144,512]{1,0:T(8,128)(2,1)S(1)}, u32[]{:S(2)}, u32[]{:S(2)}) collective-permute-start(bf16[144,512]{1,0:T(8,128)(2,1)S(1)} %pad_maximum_fusion.1), channel_id=1, source_target_pairs={{64,0},{128,64},{192,128},{256,192},{320,256},{384,320},{448,384},... | collective-permute-start | bytes 442376 | tf_op jit(solution)/shard_map/ppermute | solution.py:210
  7.5 0.1 fusion.7
  7.6 0.0 copy-done
  7.6 0.0 copy-start.6
  7.7 0.0 copy-start.1
  7.7 0.1 fusion.4
  7.8 0.5 copy-done.6
  8.3 0.0 copy-start.7
  8.3 0.6 copy-done.7
  9.0 0.0 copy-done.1
  9.0 0.1 add_convert_fusion
  9.0 0.1 fusion.6
  9.2 0.2 exponential_reduce_fusion.1
  9.4 0.1 select_maximum_fusion.1
  9.4 0.1 copy.41
  9.6 0.1 copy.40
  9.7 0.0 collective-permute-done.low_ref
  9.7 0.0 copy-start.2
  9.7 0.1 fusion.9
  9.8 0.1 copy.37
  9.9 0.1 copy.33
  10.0 3.5 %collective-permute-done.1.high_ref = bf16[144,512]{1,0:T(8,128)(2,1)S(1)} collective-permute-done((bf16[144,512]{1,0:T(8,128)(2,1)S(1)}, bf16[144,512]{1,0:T(8,128)(2,1)S(1)}, u32[]{:S(2)}, u32[]{:S(2)}) %collective-permute-start.1) | collective-permute-done | bytes 147488 | tf_op jit(solution)/shard_map/ppermute | solution.py:210
  13.5 0.1 fusion.10
  13.6 0.1 copy.38
  13.7 0.1 copy.34
  13.8 0.1 pad_maximum_fusion.5
  13.9 0.1 copy.39
  14.0 0.1 pad_maximum_fusion.4
  14.2 0.1 copy.35
  14.3 0.0 copy-done.2
  14.3 0.1 fusion.12
  14.4 0.0 copy-done.3
  14.4 0.1 fusion.11
  14.5 0.1 concatenate.47
  14.6 6.5 %collective-permute-start.2 = (bf16[464,128]{1,0:T(8,128)(2,1)S(1)}, bf16[464,128]{1,0:T(8,128)(2,1)S(1)}, u32[]{:S(2)}, u32[]{:S(2)}) collective-permute-start(bf16[464,128]{1,0:T(8,128)(2,1)S(1)} %pad_maximum_fusion.2), channel_id=1, source_target_pairs={{0,1},{1,2},{2,3},{3,4},{4,5},{5,6},{6,7},{7,8},{8,9},{9,10},{10,1... | collective-permute-start | bytes 356360 | tf_op jit(solution)/shard_map/ppermute | solution.py:210
  21.2 0.1 concatenate.52
  21.3 1.9 %collective-permute-start.3 = (bf16[464,128]{1,0:T(8,128)(2,1)S(1)}, bf16[464,128]{1,0:T(8,128)(2,1)S(1)}, u32[]{:S(2)}, u32[]{:S(2)}) collective-permute-start(bf16[464,128]{1,0:T(8,128)(2,1)S(1)} %pad_maximum_fusion.3), channel_id=1, source_target_pairs={{1,0},{2,1},{3,2},{4,3},{5,4},{6,5},{7,6},{8,7},{9,8},{10,9},{11,1... | collective-permute-start | bytes 356360 | tf_op jit(solution)/shard_map/ppermute | solution.py:210
  23.3 0.1 select_maximum_fusion.2
  23.3 0.6 select_maximum_fusion.tables_ref
  23.9 0.0 collective-permute-done.2.left_ref
  23.9 7.2 %collective-permute-done.3.right_ref = bf16[464,128]{1,0:T(8,128)(2,1)S(1)} collective-permute-done((bf16[464,128]{1,0:T(8,128)(2,1)S(1)}, bf16[464,128]{1,0:T(8,128)(2,1)S(1)}, u32[]{:S(2)}, u32[]{:S(2)}) %collective-permute-start.3) | collective-permute-done | bytes 118816 | tf_op jit(solution)/shard_map/ppermute | solution.py:210
  31.1 0.0 copy-done.4
  31.1 0.7 copy-done.5
  31.8 47.7 %smooth.1 = bf16[4,256,512]{2,1,0:T(8,128)(2,1)} custom-call(f32[8,128]{1,0:T(8,128)} %select_maximum_fusion.tables_ref, bf16[4,256,512]{2,1,0:T(8,128)(2,1)} %heights_ref.1, bf16[144,512]{1,0:T(8,128)(2,1)} %copy-done.2, bf16[144,512]{1,0:T(8,128)(2,1)} %copy-done.3, bf16[464,128]{1,0:T(8,128)(2,1)} %copy-done.4, bf16[464,128]{1,0:T(8,128)(2,1)} %copy-done.5, ...), custom_call_target="tpu_custom_call" | custom-call | tf_op jit(solution)/shard_map/smooth/pallas_call | solution.py:240
  (16 shorter events, 0.2 us)
Async XLA Ops:
  0.0 7.6 %copy-start = (bf16[4,256,512]{2,1,0:T(8,128)(2,1)S(1)}, bf16[4,256,512]{2,1,0:T(8,128)(2,1)}, u32[]{:S(2)}) copy-start(bf16[4,256,512]{2,1,0:T(8,128)(2,1)} %heights_ref.1) | copy-start | bytes 3145732
  2.2 7.5 %collective-permute-start = (bf16[144,512]{1,0:T(8,128)(2,1)S(1)}, bf16[144,512]{1,0:T(8,128)(2,1)S(1)}, u32[]{:S(2)}, u32[]{:S(2)}) collective-permute-start(bf16[144,512]{1,0:T(8,128)(2,1)S(1)} %pad_maximum_fusion), channel_id=1, source_target_pairs={{0,64},{64,128},{128,192},{192,256},{256,320},{320,384},{384,448},... | collective-permute-start | bytes 442376 | tf_op jit(solution)/shard_map/ppermute | solution.py:210
  5.1 8.5 %collective-permute-start.1 = (bf16[144,512]{1,0:T(8,128)(2,1)S(1)}, bf16[144,512]{1,0:T(8,128)(2,1)S(1)}, u32[]{:S(2)}, u32[]{:S(2)}) collective-permute-start(bf16[144,512]{1,0:T(8,128)(2,1)S(1)} %pad_maximum_fusion.1), channel_id=1, source_target_pairs={{64,0},{128,64},{192,128},{256,192},{320,256},{384,320},{448,384},... | collective-permute-start | bytes 442376 | tf_op jit(solution)/shard_map/ppermute | solution.py:210
  7.6 0.7 copy-start.6
  7.7 1.3 %copy-start.1 = (s32[256,512]{1,0:T(8,128)S(1)}, s32[256,512]{1,0:T(8,128)}, u32[]{:S(2)}) copy-start(s32[256,512]{1,0:T(8,128)} %window_ref.1) | copy-start | bytes 1572868
  8.3 0.7 copy-start.7
  9.7 4.6 %copy-start.2 = (bf16[144,512]{1,0:T(8,128)(2,1)}, bf16[144,512]{1,0:T(8,128)(2,1)S(1)}, u32[]{:S(2)}) copy-start(bf16[144,512]{1,0:T(8,128)(2,1)S(1)} %collective-permute-done.low_ref) | copy-start | bytes 442372
  13.5 0.8 %copy-start.3 = (bf16[144,512]{1,0:T(8,128)(2,1)}, bf16[144,512]{1,0:T(8,128)(2,1)S(1)}, u32[]{:S(2)}) copy-start(bf16[144,512]{1,0:T(8,128)(2,1)S(1)} %collective-permute-done.1.high_ref) | copy-start | bytes 442372
  14.6 9.3 %collective-permute-start.2 = (bf16[464,128]{1,0:T(8,128)(2,1)S(1)}, bf16[464,128]{1,0:T(8,128)(2,1)S(1)}, u32[]{:S(2)}, u32[]{:S(2)}) collective-permute-start(bf16[464,128]{1,0:T(8,128)(2,1)S(1)} %pad_maximum_fusion.2), channel_id=1, source_target_pairs={{0,1},{1,2},{2,3},{3,4},{4,5},{5,6},{6,7},{7,8},{8,9},{9,10},{10,1... | collective-permute-start | bytes 356360 | tf_op jit(solution)/shard_map/ppermute | solution.py:210
  21.3 9.8 %collective-permute-start.3 = (bf16[464,128]{1,0:T(8,128)(2,1)S(1)}, bf16[464,128]{1,0:T(8,128)(2,1)S(1)}, u32[]{:S(2)}, u32[]{:S(2)}) collective-permute-start(bf16[464,128]{1,0:T(8,128)(2,1)S(1)} %pad_maximum_fusion.3), channel_id=1, source_target_pairs={{1,0},{2,1},{3,2},{4,3},{5,4},{6,5},{7,6},{8,7},{9,8},{10,9},{11,1... | collective-permute-start | bytes 356360 | tf_op jit(solution)/shard_map/ppermute | solution.py:210
  23.9 7.2 %copy-start.4 = (bf16[464,128]{1,0:T(8,128)(2,1)}, bf16[464,128]{1,0:T(8,128)(2,1)S(1)}, u32[]{:S(2)}) copy-start(bf16[464,128]{1,0:T(8,128)(2,1)S(1)} %collective-permute-done.2.left_ref) | copy-start | bytes 356356
  31.1 0.7 copy-start.5

commit v2 on v1

--- a/solution.py
+++ b/solution.py
@@ -18,6 +18,7 @@
 FULL = ROWS + 2 * WIDE
 BROAD = COLS + 2 * RADIUS
 CODES = TALL // 2
+UNROLL = 4
 
 
 def lookup(table, codes):
@@ -39,12 +40,11 @@
     return [total * scale for total in totals]
 
 
-def smooth_blocks(source_ref, blocks, lead, code_ref, code_block, q_tab, s_tab, out_ref, length, rounded=False):
+def smooth_blocks(source_ref, blocks, lead, q_ref, s_ref, cell_block, out_ref, length, rounded=False):
     def tile(step, _):
         start = pl.multiple_of(step * 8, 8)
-        codes = code_ref[code_block, pl.ds(start, 8), :]
-        q = lookup(q_tab, codes)
-        scale = lookup(s_tab, codes)
+        q = q_ref[cell_block, pl.ds(start, 8), :]
+        scale = s_ref[cell_block, pl.ds(start, 8), :]
 
         def reader(block):
             return lambda k: source_ref[block, pl.ds(start + lead + k, 8), :]
@@ -56,17 +56,17 @@
             out_ref[block, pl.ds(start, 8), :] = result
         return 0
 
-    lax.fori_loop(0, length // 8, tile, 0, unroll=2)
+    lax.fori_loop(0, length // 8, tile, 0, unroll=UNROLL)
 
 
 def kernel(
     tables_ref, heights_ref, low_ref, high_ref, left_ref, right_ref, sigma_ref, window_ref, out_ref,
-    rows_in, rows_out, cols_in, cols_out, sig_row, sig_col, win_row, win_col,
+    rows_in, rows_out, cols_in, cols_out, q_sig, s_sig, q_sig_t, s_sig_t, q_win, s_win, q_win_t, s_win_t,
 ):
-    q_sig = tables_ref[0:1, :]
-    s_sig = tables_ref[1:2, :]
-    q_win = tables_ref[2:3, :]
-    s_win = tables_ref[3:4, :]
+    q_sig_tab = tables_ref[0:1, :]
+    s_sig_tab = tables_ref[1:2, :]
+    q_win_tab = tables_ref[2:3, :]
+    s_win_tab = tables_ref[3:4, :]
 
     for b in range(BANDS):
         for j in range(COLBLK):
@@ -78,45 +78,53 @@
     rows_in[16, :, :] = left_ref[0:FULL, :].astype(jnp.float32)
     rows_in[17, :, :] = right_ref[0:FULL, :].astype(jnp.float32)
 
+    def fill(q_ref, s_ref, block, rows, codes, q_tab, s_tab):
+        codes = codes.astype(jnp.float32).astype(jnp.int32) if codes.dtype == jnp.bfloat16 else codes
+        q_ref[block, rows, :] = lookup(q_tab, codes)
+        s_ref[block, rows, :] = lookup(s_tab, codes)
+
     for j in range(COLBLK):
         lanes = slice(j * LANES, (j + 1) * LANES)
         edge = slice(BANDS * WIDE, BANDS * WIDE + RADIUS)
-        sig_row[j, 0:RADIUS, :] = low_ref[edge, lanes].astype(jnp.float32).astype(jnp.int32)
-        sig_row[j, RADIUS:RADIUS + ROWS, :] = sigma_ref[:, lanes] + 1
-        sig_row[j, RADIUS + ROWS:TALL, :] = high_ref[edge, lanes].astype(jnp.float32).astype(jnp.int32)
-        win_row[j, :, :] = window_ref[:, lanes] + 1
+        fill(q_sig, s_sig, j, slice(0, RADIUS), low_ref[edge, lanes], q_sig_tab, s_sig_tab)
+        fill(q_sig, s_sig, j, slice(RADIUS, RADIUS + ROWS), sigma_ref[:, lanes] + 1, q_sig_tab, s_sig_tab)
+        fill(q_sig, s_sig, j, slice(RADIUS + ROWS, TALL), high_ref[edge, lanes], q_sig_tab, s_sig_tab)
+        fill(q_win, s_win, j, slice(0, ROWS), window_ref[:, lanes] + 1, q_win_tab, s_win_tab)
     halves = []
     for side, ref in ((4, left_ref), (5, right_ref)):
         packed = ref[FULL:FULL + CODES, :].astype(jnp.float32).astype(jnp.int32)
         for half in range(2):
             piece = packed[:, half * WIDE:(half + 1) * WIDE]
-            sig_row[side, half * CODES:(half + 1) * CODES, :] = jnp.concatenate([piece] * BANDS, axis=1)
+            rows = slice(half * CODES, (half + 1) * CODES)
+            fill(q_sig, s_sig, side, rows, jnp.concatenate([piece] * BANDS, axis=1), q_sig_tab, s_sig_tab)
         halves.append([packed[0:LANES, 2 * WIDE + h * RADIUS:2 * WIDE + (h + 1) * RADIUS] for h in range(2)])
     for half in range(2):
         pair = [halves[0][half], halves[1][half]]
-        win_row[4, half * LANES:(half + 1) * LANES, :] = jnp.concatenate(pair * BANDS, axis=1)
-
-    for j in range(COLBLK):
-        for i in range(ROWBLK):
-            body = sig_row[j, RADIUS + i * LANES:RADIUS + (i + 1) * LANES, :]
-            sig_col[i, RADIUS + j * LANES:RADIUS + (j + 1) * LANES, :] = body.T
-            win_col[i, j * LANES:(j + 1) * LANES, :] = win_row[j, i * LANES:(i + 1) * LANES, :].T
-        edges = jnp.concatenate([sig_row[j, 0:RADIUS, :], sig_row[j, RADIUS + ROWS:TALL, :]] * BANDS, axis=0)
-        sig_col[2, RADIUS + j * LANES:RADIUS + (j + 1) * LANES, :] = edges.T
-    for side, block in enumerate((4, 5)):
-        inner = slice(RADIUS, WIDE) if side == 0 else slice(0, RADIUS)
-        place = slice(0, RADIUS) if side == 0 else slice(RADIUS + COLS, BROAD)
-        for i in range(ROWBLK):
-            body = sig_row[block, RADIUS + i * LANES:RADIUS + (i + 1) * LANES, :].T
-            sig_col[i, place, :] = body[inner, :]
-        edges = jnp.concatenate([sig_row[block, 0:RADIUS, :], sig_row[block, RADIUS + ROWS:TALL, :]] * BANDS, axis=0)
-        sig_col[2, place, :] = edges.T[inner, :]
+        rows = slice(half * LANES, (half + 1) * LANES)
+        fill(q_win, s_win, 4, rows, jnp.concatenate(pair * BANDS, axis=1), q_win_tab, s_win_tab)
+
+    for sig_row, sig_col, win_row, win_col in ((q_sig, q_sig_t, q_win, q_win_t), (s_sig, s_sig_t, s_win, s_win_t)):
+        for j in range(COLBLK):
+            for i in range(ROWBLK):
+                body = sig_row[j, RADIUS + i * LANES:RADIUS + (i + 1) * LANES, :]
+                sig_col[i, RADIUS + j * LANES:RADIUS + (j + 1) * LANES, :] = body.T
+                win_col[i, j * LANES:(j + 1) * LANES, :] = win_row[j, i * LANES:(i + 1) * LANES, :].T
+            edges = jnp.concatenate([sig_row[j, 0:RADIUS, :], sig_row[j, RADIUS + ROWS:TALL, :]] * BANDS, axis=0)
+            sig_col[2, RADIUS + j * LANES:RADIUS + (j + 1) * LANES, :] = edges.T
+        for side, block in enumerate((4, 5)):
+            inner = slice(RADIUS, WIDE) if side == 0 else slice(0, RADIUS)
+            place = slice(0, RADIUS) if side == 0 else slice(RADIUS + COLS, BROAD)
+            for i in range(ROWBLK):
+                body = sig_row[block, RADIUS + i * LANES:RADIUS + (i + 1) * LANES, :].T
+                sig_col[i, place, :] = body[inner, :]
+            edges = jnp.concatenate([sig_row[block, 0:RADIUS, :], sig_row[block, RADIUS + ROWS:TALL, :]] * BANDS, axis=0)
+            sig_col[2, place, :] = edges.T[inner, :]
 
     for j in range(COLBLK):
         blocks = [b * COLBLK + j for b in range(BANDS)]
-        smooth_blocks(rows_in, blocks, RADIUS, sig_row, j, q_sig, s_sig, rows_out, TALL)
+        smooth_blocks(rows_in, blocks, RADIUS, q_sig, s_sig, j, rows_out, TALL)
     for side in range(2):
-        smooth_blocks(rows_in, [16 + side], RADIUS, sig_row, 4 + side, q_sig, s_sig, rows_out, TALL)
+        smooth_blocks(rows_in, [16 + side], RADIUS, q_sig, s_sig, 4 + side, rows_out, TALL)
 
     for j in range(COLBLK):
         place = slice(WIDE + j * LANES, WIDE + (j + 1) * LANES)
@@ -145,8 +153,8 @@
 
     for i in range(ROWBLK):
         blocks = [b * ROWBLK + i for b in range(BANDS)]
-        smooth_blocks(cols_in, blocks, RADIUS, sig_col, i, q_sig, s_sig, cols_out, BROAD, True)
-    smooth_blocks(cols_in, [8], RADIUS, sig_col, 2, q_sig, s_sig, cols_out, BROAD, True)
+        smooth_blocks(cols_in, blocks, RADIUS, q_sig_t, s_sig_t, i, cols_out, BROAD, True)
+    smooth_blocks(cols_in, [8], RADIUS, q_sig_t, s_sig_t, 2, cols_out, BROAD, True)
 
     for j in range(COLBLK):
         place = slice(RADIUS + j * LANES, RADIUS + (j + 1) * LANES)
@@ -172,8 +180,8 @@
 
     for j in range(COLBLK):
         blocks = [b * COLBLK + j for b in range(BANDS)]
-        smooth_blocks(rows_in, blocks, RADIUS, win_row, j, q_win, s_win, rows_out, ROWS)
-    smooth_blocks(rows_in, [16], RADIUS, win_row, 4, q_win, s_win, rows_out, ROWS)
+        smooth_blocks(rows_in, blocks, RADIUS, q_win, s_win, j, rows_out, ROWS)
+    smooth_blocks(rows_in, [16], RADIUS, q_win, s_win, 4, rows_out, ROWS)
 
     for i in range(ROWBLK):
         for j in range(COLBLK):
@@ -187,7 +195,7 @@
 
     for i in range(ROWBLK):
         blocks = [b * ROWBLK + i for b in range(BANDS)]
-        smooth_blocks(cols_in, blocks, RADIUS, win_col, i, q_win, s_win, cols_out, COLS)
+        smooth_blocks(cols_in, blocks, RADIUS, q_win_t, s_win_t, i, cols_out, COLS)
 
     for b in range(BANDS):
         for i in range(ROWBLK):
@@ -205,9 +213,15 @@
 
 def exchange(low_edge, high_edge, axis):
     count = lax.axis_size(axis)
-    forward = [(i, i + 1) for i in range(count - 1)]
-    backward = [(target, source) for source, target in forward]
-    return lax.ppermute(high_edge, axis, forward), lax.ppermute(low_edge, axis, backward)
+    even = lax.axis_index(axis) % 2 == 0
+
+    def swap(first):
+        pairs = [(i, i + 1) for i in range(first, count - 1, 2)]
+        return pairs + [(target, source) for source, target in pairs]
+
+    near = lax.ppermute(jnp.where(even, high_edge, low_edge), axis, swap(0))
+    far = lax.ppermute(jnp.where(even, low_edge, high_edge), axis, swap(1))
+    return jnp.where(even, far, near), jnp.where(even, near, far)
 
 
 def per_device(heights, sigma_class, window_class, sigma_table, window_table):
@@ -247,10 +261,14 @@
             pltpu.VMEM((18, TALL, LANES), jnp.float32),
             pltpu.VMEM((9, COLS + 2 * WIDE, LANES), jnp.float32),
             pltpu.VMEM((9, BROAD, LANES), jnp.float32),
-            pltpu.VMEM((6, TALL, LANES), jnp.int32),
-            pltpu.VMEM((3, BROAD, LANES), jnp.int32),
-            pltpu.VMEM((5, ROWS, LANES), jnp.int32),
-            pltpu.VMEM((2, COLS, LANES), jnp.int32),
+            pltpu.VMEM((6, TALL, LANES), jnp.float32),
+            pltpu.VMEM((6, TALL, LANES), jnp.float32),
+            pltpu.VMEM((3, BROAD, LANES), jnp.float32),
+            pltpu.VMEM((3, BROAD, LANES), jnp.float32),
+            pltpu.VMEM((5, ROWS, LANES), jnp.float32),
+            pltpu.VMEM((5, ROWS, LANES), jnp.float32),
+            pltpu.VMEM((2, COLS, LANES), jnp.float32),
+            pltpu.VMEM((2, COLS, LANES), jnp.float32),
         ],
         name="smooth",
     )(tables, heights, low, high, left, right, sigma_class, window_class)

time: 79.7 us -> 61.7 us (0.77)
  the two profiles are of different devices: /device:TPU:247 before, /device:TPU:3 now
where the time goes in v2:
time: 61.7 us; the launch traced here: 61.5 us
  Pallas kernels  31.4 us (51%)
  starting transfers between devices  16.8 us (27%)
  waiting for transfers between devices  5.39 us (9%)
  local copies, waits for them, and re-layouts  4.32 us (7%)
  other arithmetic  3.31 us (5%)
    pallas_call x1, Pallas kernels, per_device(): pl.pallas_call(kernel, out_shape=jax.ShapeDtypeStruct((BANDS, ROWS, COLS)...  31.4 us
    ppermute x2, starting transfers between devices, exchange(): near = lax.ppermute(jnp.where(even, high_edge, low_edge), axis, swap(0))  10.9 us
    ppermute x2, starting transfers between devices, exchange(): far = lax.ppermute(jnp.where(even, low_edge, high_edge), axis, swap(1))  5.95 us
    ppermute x2, waiting for transfers between devices, exchange(): far = lax.ppermute(jnp.where(even, low_edge, high_edge), axis, swap(1))  5.39 us
    unnamed x14, local copies, waits for them, and re-layouts  1.92 us
  transfers between devices with their start and end apart: 4, of which 2 were waited for; matrix products, arithmetic and copies ran while one was open for 3% of the time, Pallas kernels for 0%

profile of v2, /device:TPU:3, one launch (start us, length us, event | category | flops | bytes accessed | tf_op | source)
XLA Modules:
  0.0 61.5 jit_solution(2967157099409067738)
XLA Ops:
  0.0 0.0 copy-start
  0.0 1.2 %add_convert_fusion.1 = bf16[256,512]{1,0:T(8,128)(2,1)S(1)} fusion(s32[256,512]{1,0:T(8,128)} %sigma_ref.1), kind=kLoop, calls=%fused_computation.1 | loop fusion | flops 262144 | bytes 786432 | tf_op jit(solution)/shard_map/convert_element_type | solution.py:230
  1.2 1.0 %fusion.5 = (bf16[4,32,512]{2,1,0:T(8,128)(2,1)S(1)}, bf16[4,32,512]{2,1,0:T(8,128)(2,1)S(1)}) fusion(bf16[4,256,512]{2,1,0:T(8,128)(2,1)} %heights_ref.1), kind=kLoop, calls=%fused_computation.43 | loop fusion | bytes 524288 | tf_op jit(solution)/shard_map/slice | solution.py:234
  2.2 0.1 broadcast_select_fusion.2
  2.3 1.9 %collective-permute-start.1 = (bf16[144,512]{1,0:T(8,128)(2,1)S(1)}, bf16[144,512]{1,0:T(8,128)(2,1)S(1)}, u32[]{:S(2)}, u32[]{:S(2)}) collective-permute-start(bf16[144,512]{1,0:T(8,128)(2,1)S(1)} %get-tuple-element.17), channel_id=1, source_target_pairs={{0,64},{128,192},{256,320},{384,448},{64,0},{192,128},{320,256},{4... | collective-permute-start | bytes 442376 | tf_op jit(solution)/shard_map/ppermute | solution.py:222
  4.2 4.0 %collective-permute-start = (bf16[144,512]{1,0:T(8,128)(2,1)S(1)}, bf16[144,512]{1,0:T(8,128)(2,1)S(1)}, u32[]{:S(2)}, u32[]{:S(2)}) collective-permute-start(bf16[144,512]{1,0:T(8,128)(2,1)S(1)} %get-tuple-element.18), channel_id=1, source_target_pairs={{64,128},{192,256},{320,384},{128,64},{256,192},{384,320},{65,129}... | collective-permute-start | bytes 442376 | tf_op jit(solution)/shard_map/ppermute | solution.py:223
  8.2 0.1 fusion.7
  8.3 0.0 copy-done
  8.3 0.0 copy-start.4
  8.3 0.0 copy-start.1
  8.4 0.1 fusion.4
  8.5 0.5 copy-done.4
  9.0 0.0 copy-start.5
  9.0 0.6 %copy-done.5 = f32[16]{0:T(128)S(1)} copy-done((f32[16]{0:T(128)S(1)}, f32[16]{0:T(128)}, u32[]{:S(2)}) %copy-start.5) | copy-done | bytes 88
  9.7 0.0 copy-done.1
  9.7 0.1 add_convert_fusion
  9.7 0.1 fusion.6
  9.8 0.2 exponential_reduce_fusion.1
  10.0 0.1 select_maximum_fusion.1
  10.1 0.1 copy.40
  10.2 0.1 copy.41
  10.4 0.0 collective-permute-done.1
  10.4 0.3 collective-permute-done
  10.8 0.0 copy-start.2
  10.8 0.0 copy-start.3
  10.8 0.1 fusion.11
  10.9 0.1 fusion.9
  11.0 0.5 copy-done.2
  11.4 0.0 copy-done.3
  11.5 0.1 copy.33
  11.6 0.1 copy.37
  11.7 0.1 copy.38
  11.8 0.1 copy.34
  11.8 0.1 pad_maximum_fusion.4
  12.0 0.1 copy.35
  12.1 0.1 pad_maximum_fusion.5
  12.2 0.1 copy.39
  12.4 0.1 concatenate.47
  12.5 0.1 concatenate.52
  12.7 0.1 broadcast_select_fusion.6
  12.7 8.9 %collective-permute-start.3 = (bf16[464,128]{1,0:T(8,128)(2,1)S(1)}, bf16[464,128]{1,0:T(8,128)(2,1)S(1)}, u32[]{:S(2)}, u32[]{:S(2)}) collective-permute-start(bf16[464,128]{1,0:T(8,128)(2,1)S(1)} %get-tuple-element.27), channel_id=1, source_target_pairs={{0,1},{2,3},{4,5},{6,7},{8,9},{10,11},{12,13},{14,15},{16,17},{18,... | collective-permute-start | bytes 356360 | tf_op jit(solution)/shard_map/ppermute | solution.py:222
  21.7 1.9 %collective-permute-start.2 = (bf16[464,128]{1,0:T(8,128)(2,1)S(1)}, bf16[464,128]{1,0:T(8,128)(2,1)S(1)}, u32[]{:S(2)}, u32[]{:S(2)}) collective-permute-start(bf16[464,128]{1,0:T(8,128)(2,1)S(1)} %get-tuple-element.28), channel_id=1, source_target_pairs={{1,2},{3,4},{5,6},{7,8},{9,10},{11,12},{13,14},{15,16},{17,18},{19... | collective-permute-start | bytes 356360 | tf_op jit(solution)/shard_map/ppermute | solution.py:223
  23.6 0.1 select_maximum_fusion.2
  23.7 0.6 select_maximum_fusion.tables_ref
  24.3 0.0 collective-permute-done.3
  24.3 5.0 %collective-permute-done.2 = bf16[464,128]{1,0:T(8,128)(2,1)S(1)} collective-permute-done((bf16[464,128]{1,0:T(8,128)(2,1)S(1)}, bf16[464,128]{1,0:T(8,128)(2,1)S(1)}, u32[]{:S(2)}, u32[]{:S(2)}) %collective-permute-start.2) | collective-permute-done | bytes 118816 | tf_op jit(solution)/shard_map/ppermute | solution.py:223
  29.3 0.7 %broadcast_select_fusion.4 = (bf16[464,128]{1,0:T(8,128)(2,1)}, bf16[464,128]{1,0:T(8,128)(2,1)}) fusion(bf16[464,128]{1,0:T(8,128)(2,1)S(1)} %collective-permute-done.3, bf16[464,128]{1,0:T(8,128)(2,1)S(1)} %collective-permute-done.2, pred[]{:T(512)S(6)} %eq.10), kind=kLoop, calls=%fused_computation.10 | loop fusion | flops 118784 | bytes 475137 | tf_op jit(solution)/shard_map/jit(_where)/select_n | solution.py:224
  30.1 31.4 %smooth.1 = bf16[4,256,512]{2,1,0:T(8,128)(2,1)} custom-call(f32[8,128]{1,0:T(8,128)} %select_maximum_fusion.tables_ref, bf16[4,256,512]{2,1,0:T(8,128)(2,1)} %heights_ref.1, bf16[144,512]{1,0:T(8,128)(2,1)} %copy-done.3, bf16[144,512]{1,0:T(8,128)(2,1)} %copy-done.2, bf16[464,128]{1,0:T(8,128)(2,1)} %get-tuple-element.26.left_ref, ...), custom_call_target="tpu_custom_call" | custom-call | tf_op jit(solution)/shard_map/smooth/pallas_call | solution.py:254
  (11 shorter events, 0.1 us)
Async XLA Ops:
  0.0 8.3 %copy-start = (bf16[4,256,512]{2,1,0:T(8,128)(2,1)S(1)}, bf16[4,256,512]{2,1,0:T(8,128)(2,1)}, u32[]{:S(2)}) copy-start(bf16[4,256,512]{2,1,0:T(8,128)(2,1)} %heights_ref.1) | copy-start | bytes 3145732
  2.3 8.1 %collective-permute-start.1 = (bf16[144,512]{1,0:T(8,128)(2,1)S(1)}, bf16[144,512]{1,0:T(8,128)(2,1)S(1)}, u32[]{:S(2)}, u32[]{:S(2)}) collective-permute-start(bf16[144,512]{1,0:T(8,128)(2,1)S(1)} %get-tuple-element.17), channel_id=1, source_target_pairs={{0,64},{128,192},{256,320},{384,448},{64,0},{192,128},{320,256},{4... | collective-permute-start | bytes 442376 | tf_op jit(solution)/shard_map/ppermute | solution.py:222
  4.2 6.5 %collective-permute-start = (bf16[144,512]{1,0:T(8,128)(2,1)S(1)}, bf16[144,512]{1,0:T(8,128)(2,1)S(1)}, u32[]{:S(2)}, u32[]{:S(2)}) collective-permute-start(bf16[144,512]{1,0:T(8,128)(2,1)S(1)} %get-tuple-element.18), channel_id=1, source_target_pairs={{64,128},{192,256},{320,384},{128,64},{256,192},{384,320},{65,129}... | collective-permute-start | bytes 442376 | tf_op jit(solution)/shard_map/ppermute | solution.py:223
  8.3 0.7 %copy-start.4 = (f32[16]{0:T(128)S(1)}, f32[16]{0:T(128)}, u32[]{:S(2)}) copy-start(f32[16]{0:T(128)} %param.8) | copy-start | bytes 196
  8.3 1.3 %copy-start.1 = (s32[256,512]{1,0:T(8,128)S(1)}, s32[256,512]{1,0:T(8,128)}, u32[]{:S(2)}) copy-start(s32[256,512]{1,0:T(8,128)} %window_ref.1) | copy-start | bytes 1572868
  9.0 0.7 %copy-start.5 = (f32[16]{0:T(128)S(1)}, f32[16]{0:T(128)}, u32[]{:S(2)}) copy-start(f32[16]{0:T(128)} %param.9) | copy-start | bytes 196
  10.8 0.7 %copy-start.2 = (bf16[144,512]{1,0:T(8,128)(2,1)}, bf16[144,512]{1,0:T(8,128)(2,1)S(1)}, u32[]{:S(2)}) copy-start(bf16[144,512]{1,0:T(8,128)(2,1)S(1)} %get-tuple-element.15.high_ref) | copy-start | bytes 442372
  10.8 0.7 %copy-start.3 = (bf16[144,512]{1,0:T(8,128)(2,1)}, bf16[144,512]{1,0:T(8,128)(2,1)S(1)}, u32[]{:S(2)}) copy-start(bf16[144,512]{1,0:T(8,128)(2,1)S(1)} %get-tuple-element.16.low_ref) | copy-start | bytes 442372
  12.7 11.6 %collective-permute-start.3 = (bf16[464,128]{1,0:T(8,128)(2,1)S(1)}, bf16[464,128]{1,0:T(8,128)(2,1)S(1)}, u32[]{:S(2)}, u32[]{:S(2)}) collective-permute-start(bf16[464,128]{1,0:T(8,128)(2,1)S(1)} %get-tuple-element.27), channel_id=1, source_target_pairs={{0,1},{2,3},{4,5},{6,7},{8,9},{10,11},{12,13},{14,15},{16,17},{18,... | collective-permute-start | bytes 356360 | tf_op jit(solution)/shard_map/ppermute | solution.py:222
  21.7 7.7 %collective-permute-start.2 = (bf16[464,128]{1,0:T(8,128)(2,1)S(1)}, bf16[464,128]{1,0:T(8,128)(2,1)S(1)}, u32[]{:S(2)}, u32[]{:S(2)}) collective-permute-start(bf16[464,128]{1,0:T(8,128)(2,1)S(1)} %get-tuple-element.28), channel_id=1, source_target_pairs={{1,2},{3,4},{5,6},{7,8},{9,10},{11,12},{13,14},{15,16},{17,18},{19... | collective-permute-start | bytes 356360 | tf_op jit(solution)/shard_map/ppermute | solution.py:223
